TPU v7x, 512 devices: a whole 4x8x8 slice. The times are simulated.
512 devices in a mesh: inp: 128 (over y, z, core), vis: 4 (over x).
Axes of the slice: x: 4, y: 8, z: 8, core: 2. Of those that a mesh axis runs over, the one named last changes fastest.
Arguments:
- samples: bfloat16 [128, 2048, 2048], P('vis', 'inp'), may hold values from -6 to 6
- history: bfloat16 [3, 2048, 2048], P(None, 'inp'), may hold values from -6 to 6
- fir_taps: float32 [4, 2048], replicated, may hold values from -3 to 3
- kept_channels: int32 [128], replicated, may hold values from 0 to 1023, as said below
Outputs:
- visibility: bfloat16 [128, 2048, 2048], P('inp', 'vis')
Inputs may be any that keep to these rules, and one draw needn't show every extreme that they name: `kept_channels`: 128 distinct channel numbers in no particular order; channels 0 and 1023 are always among them.
All inputs are finite; a program needn't handle non-finite values.
Results may differ from a plain program's by a relative error of at most 0.0078.
Values may be sent and summed in bfloat16 or wider, within the bound.
A program may use at most 64 MiB of HBM per device.

v0:
```python
from functools import partial
import math
import jax
import jax.numpy as jnp
from jax import lax
from jax.sharding import PartitionSpec as P

TAPS = 4
CH_DEV = 1


def shifted(value, axis, steps):
    count = lax.axis_size(axis)
    initial, last = (max(0, -steps), min(count, count - steps))
    return lax.ppermute(value, axis, [(source, source + steps) for source in range(initial, last)])


def make_table(kept_channels, sample_count):
    positions = jnp.arange(sample_count, dtype=jnp.int32)
    products = kept_channels[:, None] * positions[None, :] % sample_count
    angles = products.astype(jnp.float32) * (2.0 * math.pi / sample_count)
    norm_scale = 1.0 / math.sqrt(sample_count)
    table = jnp.concatenate([jnp.cos(angles) * norm_scale, -jnp.sin(angles) * norm_scale], axis=0)
    return table.astype(jnp.bfloat16)


def add_frames(running, shard_piece, offset, vis_index, row_count):
    real_part = shard_piece[0]
    imag_part = shard_piece[1]
    stacked = jnp.concatenate([real_part, imag_part], axis=1)
    rotated = jnp.concatenate([-imag_part, real_part], axis=1)
    row_block = lax.dynamic_slice_in_dim(stacked, vis_index * row_count, row_count, 2)
    input_total = stacked.shape[2]
    re_block = jnp.einsum("cfa,cfb->cab", row_block, stacked, preferred_element_type=jnp.float32)
    im_block = jnp.einsum("cfa,cfb->cab", row_block, rotated, preferred_element_type=jnp.float32)
    row_ids = vis_index * row_count + jnp.arange(row_count, dtype=jnp.int32)
    col_ids = jnp.arange(input_total, dtype=jnp.int32)
    contribution = jnp.where(col_ids[None, None, :] >= row_ids[None, :, None], re_block, im_block)
    return contribution


def per_device(samples, history, fir_taps, kept_channels):
    vis_count = lax.axis_size("vis")
    vis_index = lax.axis_index("vis")
    inp_count = lax.axis_size("inp")
    frame_count, input_count, sample_count = samples.shape
    history_len = TAPS - 1
    previous = shifted(samples[frame_count - history_len :], "vis", 1)
    previous = jnp.where(vis_index == 0, history, previous)
    extended = jnp.concatenate([previous, samples], axis=0)
    weighted = fir_taps[0][None, None, :] * extended[0:frame_count].astype(jnp.float32)
    for tap_index in range(1, TAPS):
        weighted = weighted + fir_taps[tap_index][None, None, :] * extended[
            tap_index : tap_index + frame_count
        ].astype(jnp.float32)
    weighted = weighted.astype(jnp.bfloat16)
    dft_table = make_table(kept_channels, sample_count)
    kept_total = kept_channels.shape[0]
    spectra = jnp.einsum(
        "kn,fin->kfi", dft_table, weighted, preferred_element_type=jnp.float32
    ).astype(jnp.bfloat16)
    spectra = spectra.reshape(2, kept_total, frame_count, input_count)
    input_total = input_count * inp_count
    row_count = input_total // vis_count
    frame_total = frame_count * vis_count
    initial = jnp.zeros((CH_DEV, row_count, input_total), jnp.float32)
    correlate = partial(add_frames, vis_index=vis_index, row_count=row_count)
    all_frames = lax.all_gather(spectra, "vis", axis=2, tiled=True)
    channel_data = lax.all_to_all(all_frames, "inp", split_axis=1, concat_axis=3, tiled=True)
    summed = correlate(initial, channel_data, 0)
    return (summed / float(frame_total)).astype(jnp.bfloat16)


def solution(mesh):
    return jax.shard_map(
        per_device,
        mesh=mesh,
        in_specs=(P("vis", "inp", None), P(None, "inp", None), P(), P()),
        out_specs=P("inp", "vis", None),
        check_vma=False,
    )
```

profile of v0, /device:TPU:1, one launch (start us, length us, event | category | flops | bytes accessed | tf_op | source)
XLA Modules:
  0.0 116.5 jit_solution(1827298505399509753)
XLA Ops:
  6.5 0.0 copy-start
  6.5 0.0 all-gather.2.cloned.1.call-start
  6.5 1.1 slice.33
  7.6 4.0 %collective-permute-start = (bf16[3,16,2048]{2,1,0:T(8,128)(2,1)S(1)}, bf16[3,16,2048]{2,1,0:T(8,128)(2,1)S(1)}, u32[]{:S(2)}, u32[]{:S(2)}) collective-permute-start(bf16[3,16,2048]{2,1,0:T(8,128)(2,1)S(1)} %slice.33), channel_id=1, source_target_pairs={{0,1},{1,2},{2,3},{4,5},{5,6},{6,7},{8,9},{9,10},{10,11},{12,13},{... | collective-permute-start | bytes 589832 | tf_op jit(solution)/shard_map/ppermute | solution.py:15
  11.6 5.6 %multiply_convert_fusion.2 = (bf16[128,2048]{1,0:T(8,128)(2,1)S(1)}, bf16[128,2048]{1,0:T(8,128)(2,1)S(1)}) fusion(s32[128]{0:T(128)} %param.7), kind=kLoop, calls=%fused_computation.33 | loop fusion | flops 4980736 | bytes 1049088 | tf_op jit(solution)/shard_map/convert
  17.2 1.5 %fusion.29 = (f32[1,2048]{1,0:T(1,128)S(1)}, f32[1,2048]{1,0:T(1,128)S(1)}, f32[1,2048]{1,0:T(1,128)}, f32[1,2048]{1,0:T(1,128)}) fusion(f32[4,2048]{1,0:T(4,128)} %param.6), kind=kLoop, calls=%fused_computation.46 | loop fusion | bytes 65536 | tf_op jit(solution)/shard_map/slice | solution.py:51
  18.8 0.0 collective-permute-done
  18.8 1.0 broadcast_select_fusion
  19.7 0.0 copy-done
  19.7 2.7 %add_convert_fusion = bf16[32,16,2048]{2,1,0:T(8,128)(2,1)S(1)} fusion(bf16[32,16,2048]{2,1,0:T(8,128)(2,1)S(1)} %copy-done, bf16[3,16,2048]{2,1,0:T(8,128)(2,1)S(1)} %broadcast_select_fusion, f32[2048]{0:T(1024)} %bitcast.36, f32[2048]{0:T(1024)} %bitcast.37, f32[2048]{0:T(1024)S(1)} %bitcast.35, f32[2048]{0:T(1024)S(1)} %bitcast.34), kind=kLoop, calls=%fused_computation.1 | loop fusion | flops 15728640 | bytes 4423680 | tf_op jit(solution)/shard_map/convert_element_type | solution.py:56
  22.5 1.6 %fusion.5 = bf16[256,32,16]{0,1,2:T(8,128)(2,1)S(1)} fusion(bf16[32,16,2048]{2,1,0:T(8,128)(2,1)S(1)} %add_convert_fusion, bf16[128,2048]{1,0:T(8,128)(2,1)S(1)} %get-tuple-element.12, bf16[128,2048]{1,0:T(8,128)(2,1)S(1)} %get-tuple-element.11), kind=kOutput, calls=%fused_computation.16 | convolution fusion | flops 539099136 | bytes 3407872 | tf_op jit(solution)/shard_map/kn,fin->kfi/dot_general | solution.py:59
  24.1 0.1 reshape.47
  24.2 1.0 copy.9
  25.2 0.0 all-gather.2.cloned.1.call-update
  25.2 32.2 %all-gather.2.cloned.1.call-done = bf16[2,128,128,16]{1,3,0,2:T(8,128)(2,1)} async-done(((bf16[2,128,32,16]{1,3,0,2:T(8,128)(2,1)}), bf16[2,128,128,16]{1,3,0,2:T(8,128)(2,1)}) %all-gather.2.cloned.1.call-update) | async-done | bytes 1048592 | tf_op jit(solution)/shard_map/all_gather | solution.py:68
  57.5 3.2 %copy.10 = bf16[2,128,128,16]{2,3,0,1:T(8,128)(2,1)} copy(bf16[2,128,128,16]{1,3,0,2:T(8,128)(2,1)} %all-gather.2.cloned.1.call-done) | data formatting | bytes 2097152 | tf_op jit(solution)/shard_map/all_gather | solution.py:68
  60.7 15.2 %all-to-all-start = ((bf16[2,128,128,16]{2,3,0,1:T(8,128)(2,1)}), bf16[2,128,128,16]{2,3,0,1:T(8,128)(2,1)S(1)}, u32[]{:S(2)}, u32[]{:S(2)}) async-start(bf16[2,128,128,16]{2,3,0,1:T(8,128)(2,1)} %copy.10), calls=%async_computation | async-start | bytes 2097152 | tf_op jit(solution)/shard_map/all_to_all | solution.py:69
  75.9 30.4 %all-to-all-done = bf16[2,128,128,16]{2,3,0,1:T(8,128)(2,1)S(1)} async-done(((bf16[2,128,128,16]{2,3,0,1:T(8,128)(2,1)}), bf16[2,128,128,16]{2,3,0,1:T(8,128)(2,1)S(1)}, u32[]{:S(2)}, u32[]{:S(2)}) %all-to-all-start) | async-done | bytes 1048608 | tf_op jit(solution)/shard_map/all_to_all | solution.py:69
  106.3 0.2 copy.17
  106.5 0.2 fusion.28
  106.7 0.1 bitcast_negate_fusion
  106.8 0.7 fusion.9
  107.5 2.1 %fusion = bf16[1,512,2048]{2,1,0:T(8,128)(2,1)} fusion(f32[512,2048]{1,0:T(8,128)S(1)} %fusion.9, s32[512]{0:T(512)S(1)} %iota_add_fusion, bf16[1,128,2048]{1,2,0:T(8,128)(2,1)S(1)} %bitcast.30, bf16[1,128,2048]{1,2,0:T(8,128)(2,1)S(1)} %bitcast_negate_fusion, s32[]{:T(128)S(6)} %select_n.26, bf16[1,128,2048]{1,2,0:T(8,128)(2,1)S(1)} %bitcast.32), kind=kOutput, calls=%fused_computation.5 | convolution fusion | flops 543686656 | bytes 8390660 | tf_op jit(solution)/shard_map/cfa,cfb->cab/dot_general | solution.py:35
  (1 shorter events, 0.0 us)
Async XLA Ops:
  6.5 13.2 %copy-start = (bf16[32,16,2048]{2,1,0:T(8,128)(2,1)S(1)}, bf16[32,16,2048]{2,1,0:T(8,128)(2,1)}, u32[]{:S(2)}) copy-start(bf16[32,16,2048]{2,1,0:T(8,128)(2,1)} %param.4) | copy-start | bytes 6291460
  6.5 50.9 %all-gather.2.cloned.1.call-start = ((), (), s32[]{:S(2)}) async-start(), calls=%async_computation.1 | async-start | bytes 1310720 | tf_op jit(solution)/shard_map/all_gather | solution.py:68
  7.6 11.1 %collective-permute-start = (bf16[3,16,2048]{2,1,0:T(8,128)(2,1)S(1)}, bf16[3,16,2048]{2,1,0:T(8,128)(2,1)S(1)}, u32[]{:S(2)}, u32[]{:S(2)}) collective-permute-start(bf16[3,16,2048]{2,1,0:T(8,128)(2,1)S(1)} %slice.33), channel_id=1, source_target_pairs={{0,1},{1,2},{2,3},{4,5},{5,6},{6,7},{8,9},{9,10},{10,11},{12,13},{... | collective-permute-start | bytes 589832 | tf_op jit(solution)/shard_map/ppermute | solution.py:15
  60.7 45.6 %all-to-all-start = ((bf16[2,128,128,16]{2,3,0,1:T(8,128)(2,1)}), bf16[2,128,128,16]{2,3,0,1:T(8,128)(2,1)S(1)}, u32[]{:S(2)}, u32[]{:S(2)}) async-start(bf16[2,128,128,16]{2,3,0,1:T(8,128)(2,1)} %copy.10), calls=%async_computation | async-start | bytes 2097152 | tf_op jit(solution)/shard_map/all_to_all | solution.py:69
Sparse Core Ops, SparseCore 0:
  25.4 32.0 all-gather.1
where the time goes:
time: 117 us
  waiting for transfers between devices  62.7 us (54%)
  starting transfers between devices  19.2 us (16%)
  between operations  13.5 us (12%)
  other arithmetic  9.41 us (8%)
  local copies, waits for them, and re-layouts  7.24 us (6%)
  matrix products  4.52 us (4%)
    all_gather x1, waiting for transfers between devices, per_device(): all_frames = lax.all_gather(spectra, 'vis', axis=2, tiled=True)  32.2 us
    all_to_all x1, waiting for transfers between devices, per_device(): lax.all_to_all(all_frames, 'inp', split_axis=1, concat_axis=3, tiled=True)  30.4 us
    all_to_all x1, starting transfers between devices, per_device(): lax.all_to_all(all_frames, 'inp', split_axis=1, concat_axis=3, tiled=True)  15.2 us
    another operation x1, other arithmetic  5.62 us
    ppermute x1, starting transfers between devices, shifted(): lax.ppermute(value, axis, [(source, source + steps) for source in range(i...  3.96 us
    all_gather x1, local copies, waits for them, and re-layouts, per_device(): all_frames = lax.all_gather(spectra, 'vis', axis=2, tiled=True)  3.17 us
    convert_element_type x1, other arithmetic, per_device(): weighted = weighted.astype(jnp.bfloat16)  2.74 us
  transfers between devices with their start and end apart: 3, of which 2 were waited for; matrix products, arithmetic and copies ran while one was open for 6% of the time, Pallas kernels for 0%

commit v1 on v0

--- a/solution.py
+++ b/solution.py
@@ -65,7 +65,9 @@
     frame_total = frame_count * vis_count
     initial = jnp.zeros((CH_DEV, row_count, input_total), jnp.float32)
     correlate = partial(add_frames, vis_index=vis_index, row_count=row_count)
-    all_frames = lax.all_gather(spectra, "vis", axis=2, tiled=True)
+    all_frames = jnp.concatenate(
+        lax.all_to_all(jnp.stack([spectra] * lax.axis_size("vis")), "vis", 0, 0), axis=2
+    )
     channel_data = lax.all_to_all(all_frames, "inp", split_axis=1, concat_axis=3, tiled=True)
     summed = correlate(initial, channel_data, 0)
     return (summed / float(frame_total)).astype(jnp.bfloat16)

time: 117 us -> 90.2 us (0.77)
  waiting for transfers between devices: 62.7 us -> 30.4 us
  blocking collectives: 0 us -> 13.4 us
  between operations: 13.5 us -> 0.12 us
  starting transfers between devices: 19.2 us -> 26.1 us
  local copies, waits for them, and re-layouts: 7.24 us -> 5.84 us
    all_gather x1 -> x0, waiting for transfers between devices: 32.2 us -> none  [per_device(): all_frames = lax.all_gather(spectra, 'vis', axis=2, tiled=True)]
    all_to_all x0 -> x1, blocking collectives: none -> 13.4 us  [per_device(): lax.all_to_all(jnp.stack([spectra] * lax.axis_size('vis')), 'vis', 0, 0)]
    all_to_all x1, starting transfers between devices: 15.2 us -> 22.2 us  [per_device(): lax.all_to_all(all_frames, 'inp', split_axis=1, concat_axis=3, tiled=True)]
    all_gather x1 -> x0, local copies, waits for them, and re-layouts: 3.17 us -> none  [per_device(): all_frames = lax.all_gather(spectra, 'vis', axis=2, tiled=True)]
    reshape x2 -> x1, local copies, waits for them, and re-layouts: 1.08 us -> 2.26 us  [per_device(): jnp.concatenate(lax.all_to_all(jnp.stack([spectra] * lax.axis_size('vis')...]
  transfers between devices with their start and end apart: 3 -> 2, of which waited for: 2 -> 1; matrix products, arithmetic and copies ran while one was open for 6% -> 8% of each run, Pallas kernels for 0% -> 0%
where the time goes in v1:
time: 90.2 us; the launch traced here: 89.8 us
  waiting for transfers between devices  30.4 us (34%)
  starting transfers between devices  26.1 us (29%)
  blocking collectives  13.4 us (15%)
  other arithmetic  9.42 us (10%)
  local copies, waits for them, and re-layouts  5.84 us (6%)
  matrix products  4.52 us (5%)
    all_to_all x1, waiting for transfers between devices, per_device(): lax.all_to_all(all_frames, 'inp', split_axis=1, concat_axis=3, tiled=True)  30.4 us
    all_to_all x1, starting transfers between devices, per_device(): lax.all_to_all(all_frames, 'inp', split_axis=1, concat_axis=3, tiled=True)  22.2 us
    all_to_all x1, blocking collectives, per_device(): lax.all_to_all(jnp.stack([spectra] * lax.axis_size('vis')), 'vis', 0, 0)  13.4 us
    another operation x1, other arithmetic  5.62 us
    ppermute x1, starting transfers between devices, shifted(): lax.ppermute(value, axis, [(source, source + steps) for source in range(i...  3.96 us
    convert_element_type x1, other arithmetic, per_device(): weighted = weighted.astype(jnp.bfloat16)  2.75 us
    reshape x1, local copies, waits for them, and re-layouts, per_device(): jnp.concatenate(lax.all_to_all(jnp.stack([spectra] * lax.axis_size('vis')...  2.26 us
    dot_general x1, matrix products, add_frames(): jnp.einsum('cfa,cfb->cab', row_block, rotated, preferred_element_type=jnp...  2.14 us
  transfers between devices with their start and end apart: 2, of which 1 were waited for; matrix products, arithmetic and copies ran while one was open for 8% of the time, Pallas kernels for 0%

profile of v1, /device:TPU:1, one launch (start us, length us, event | category | flops | bytes accessed | tf_op | source)
XLA Modules:
  0.0 89.8 jit_solution(12733557642230645791)
XLA Ops:
  0.0 0.0 copy-start
  0.0 1.1 %slice.33 = bf16[3,16,2048]{2,1,0:T(8,128)(2,1)S(1)} slice(bf16[32,16,2048]{2,1,0:T(8,128)(2,1)} %param.4), slice={[29:32], [0:16], [0:2048]} | slice | bytes 393216 | tf_op jit(solution)/shard_map/slice | solution.py:48
  1.1 4.0 %collective-permute-start = (bf16[3,16,2048]{2,1,0:T(8,128)(2,1)S(1)}, bf16[3,16,2048]{2,1,0:T(8,128)(2,1)S(1)}, u32[]{:S(2)}, u32[]{:S(2)}) collective-permute-start(bf16[3,16,2048]{2,1,0:T(8,128)(2,1)S(1)} %slice.33), channel_id=1, source_target_pairs={{0,1},{1,2},{2,3},{4,5},{5,6},{6,7},{8,9},{9,10},{10,11},{12,13},{... | collective-permute-start | bytes 589832 | tf_op jit(solution)/shard_map/ppermute | solution.py:15
  5.1 5.6 %multiply_convert_fusion.2 = (bf16[128,2048]{1,0:T(8,128)(2,1)S(1)}, bf16[128,2048]{1,0:T(8,128)(2,1)S(1)}) fusion(s32[128]{0:T(128)} %param.7), kind=kLoop, calls=%fused_computation.33 | loop fusion | flops 4980736 | bytes 1049088 | tf_op jit(solution)/shard_map/convert
  10.7 1.6 %fusion.29 = (f32[1,2048]{1,0:T(1,128)S(1)}, f32[1,2048]{1,0:T(1,128)S(1)}, f32[1,2048]{1,0:T(1,128)}, f32[1,2048]{1,0:T(1,128)}) fusion(f32[4,2048]{1,0:T(4,128)} %param.6), kind=kLoop, calls=%fused_computation.46 | loop fusion | bytes 65536 | tf_op jit(solution)/shard_map/slice | solution.py:51
  12.3 0.0 collective-permute-done
  12.3 1.0 %broadcast_select_fusion = bf16[3,16,2048]{2,1,0:T(8,128)(2,1)S(1)} fusion(bf16[3,16,2048]{2,1,0:T(8,128)(2,1)} %param.5, bf16[3,16,2048]{2,1,0:T(8,128)(2,1)S(1)} %collective-permute-done, pred[]{:T(512)S(6)} %eq.5), kind=kLoop, calls=%fused_computation.39 | loop fusion | flops 98304 | bytes 589825 | tf_op jit(solution)/shard_map/jit(_where)/select_n | solution.py:49
  13.2 0.0 copy-done
  13.2 2.7 %add_convert_fusion = bf16[32,16,2048]{2,1,0:T(8,128)(2,1)S(1)} fusion(bf16[32,16,2048]{2,1,0:T(8,128)(2,1)S(1)} %copy-done, bf16[3,16,2048]{2,1,0:T(8,128)(2,1)S(1)} %broadcast_select_fusion, f32[2048]{0:T(1024)} %bitcast.40, f32[2048]{0:T(1024)} %bitcast.41, f32[2048]{0:T(1024)S(1)} %bitcast.39, f32[2048]{0:T(1024)S(1)} %bitcast.38), kind=kLoop, calls=%fused_computation.1 | loop fusion | flops 15728640 | bytes 4423680 | tf_op jit(solution)/shard_map/convert_element_type | solution.py:56
  16.0 1.6 %fusion.5 = bf16[256,32,16]{0,1,2:T(8,128)(2,1)S(1)} fusion(bf16[32,16,2048]{2,1,0:T(8,128)(2,1)S(1)} %add_convert_fusion, bf16[128,2048]{1,0:T(8,128)(2,1)S(1)} %get-tuple-element.12, bf16[128,2048]{1,0:T(8,128)(2,1)S(1)} %get-tuple-element.11), kind=kOutput, calls=%fused_computation.16 | convolution fusion | flops 539099136 | bytes 3407872 | tf_op jit(solution)/shard_map/kn,fin->kfi/dot_general | solution.py:59
  17.6 0.1 stack_reshape.2
  17.7 0.2 copy.17
  17.9 0.1 stack.3
  18.0 13.4 %all_to_all.20 = bf16[4,2,128,32,16]{2,4,3,1,0:T(8,128)(2,1)S(1)} all-to-all(bf16[4,2,128,32,16]{2,4,3,1,0:T(8,128)(2,1)S(1)} %stack.3), channel_id=1, replica_groups=mesh['inp'=128,'vis'=4] {'vis'}, dimensions={0} | all-to-all | bytes 2097152 | tf_op jit(solution)/shard_map/all_to_all | solution.py:69
  31.4 0.2 copy.18
  31.6 2.3 %copy.19 = bf16[2,128,128,16]{2,3,0,1:T(8,128)(2,1)} copy(bf16[2,128,128,16]{1,3,2,0:T(8,128)(2,1)S(1)} %bitcast.37) | data formatting | bytes 2097152 | tf_op jit(solution)/shard_map/reshape | solution.py:68
  33.8 22.2 %all-to-all-start.1 = ((bf16[2,128,128,16]{2,3,0,1:T(8,128)(2,1)}), bf16[2,128,128,16]{2,3,0,1:T(8,128)(2,1)S(1)}, u32[]{:S(2)}, u32[]{:S(2)}) async-start(bf16[2,128,128,16]{2,3,0,1:T(8,128)(2,1)} %copy.19), calls=%async_computation.1 | async-start | bytes 2097152 | tf_op jit(solution)/shard_map/all_to_all | solution.py:71
  56.0 30.4 %all-to-all-done.1 = bf16[2,128,128,16]{2,3,0,1:T(8,128)(2,1)S(1)} async-done(((bf16[2,128,128,16]{2,3,0,1:T(8,128)(2,1)}), bf16[2,128,128,16]{2,3,0,1:T(8,128)(2,1)S(1)}, u32[]{:S(2)}, u32[]{:S(2)}) %all-to-all-start.1) | async-done | bytes 1048608 | tf_op jit(solution)/shard_map/all_to_all | solution.py:71
  86.5 0.2 copy.26
  86.7 0.2 fusion.28
  86.8 0.1 bitcast_negate_fusion
  87.0 0.7 fusion.9
  87.7 2.1 %fusion = bf16[1,512,2048]{2,1,0:T(8,128)(2,1)} fusion(f32[512,2048]{1,0:T(8,128)S(1)} %fusion.9, s32[512]{0:T(512)S(1)} %iota_add_fusion, bf16[1,128,2048]{1,2,0:T(8,128)(2,1)S(1)} %bitcast.33, bf16[1,128,2048]{1,2,0:T(8,128)(2,1)S(1)} %bitcast_negate_fusion, s32[]{:T(128)S(6)} %select_n.26, bf16[1,128,2048]{1,2,0:T(8,128)(2,1)S(1)} %bitcast.35), kind=kOutput, calls=%fused_computation.5 | convolution fusion | flops 543686656 | bytes 8390660 | tf_op jit(solution)/shard_map/cfa,cfb->cab/dot_general | solution.py:35
  (1 shorter events, 0.0 us)
Async XLA Ops:
  0.0 13.2 %copy-start = (bf16[32,16,2048]{2,1,0:T(8,128)(2,1)S(1)}, bf16[32,16,2048]{2,1,0:T(8,128)(2,1)}, u32[]{:S(2)}) copy-start(bf16[32,16,2048]{2,1,0:T(8,128)(2,1)} %param.4) | copy-start | bytes 6291460
  1.1 11.2 %collective-permute-start = (bf16[3,16,2048]{2,1,0:T(8,128)(2,1)S(1)}, bf16[3,16,2048]{2,1,0:T(8,128)(2,1)S(1)}, u32[]{:S(2)}, u32[]{:S(2)}) collective-permute-start(bf16[3,16,2048]{2,1,0:T(8,128)(2,1)S(1)} %slice.33), channel_id=1, source_target_pairs={{0,1},{1,2},{2,3},{4,5},{5,6},{6,7},{8,9},{9,10},{10,11},{12,13},{... | collective-permute-start | bytes 589832 | tf_op jit(solution)/shard_map/ppermute | solution.py:15
  33.8 52.6 %all-to-all-start.1 = ((bf16[2,128,128,16]{2,3,0,1:T(8,128)(2,1)}), bf16[2,128,128,16]{2,3,0,1:T(8,128)(2,1)S(1)}, u32[]{:S(2)}, u32[]{:S(2)}) async-start(bf16[2,128,128,16]{2,3,0,1:T(8,128)(2,1)} %copy.19), calls=%async_computation.1 | async-start | bytes 2097152 | tf_op jit(solution)/shard_map/all_to_all | solution.py:71
